TPU v7x, 256 devices: a whole 4x4x8 slice. The times are simulated.
256 devices in a mesh: section: 8 (over y, core), shard: 32 (over z, x).
Axes of the slice: x: 4, y: 4, z: 8, core: 2. Of those that a mesh axis runs over, the one named last changes fastest.
Arguments:
- activations: bfloat16 [8, 8, 32, 8192], P('section', None, None, 'shard'), may hold values from -6 to 6
- top_grad: bfloat16 [8, 32, 8192], P(None, None, 'shard'), may hold values from -6 to 6
- projection: bfloat16 [8, 8192, 8192], P('section', None, 'shard'), may hold values from -0.03125 to 0.03125
- basis_out: bfloat16 [8, 8192, 4096], P('section', None, 'shard'), may hold values from -0.0625 to 0.0625
- basis_in: bfloat16 [8, 8192, 4096], P('section', 'shard'), may hold values from -0.0625 to 0.0625
Outputs:
- eigenvalues: float32 [8, 4096, 4096], P('section', 'shard')
All inputs are finite; a program needn't handle non-finite values.
Results may differ from a plain program's by a relative error of at most 0.007.
Values may be sent and summed in bfloat16 or wider, within the bound.
A program may use at most 64 MiB of HBM per device.

v0:
```python
import jax
import jax.numpy as jnp
from jax import lax
from jax.sharding import Mesh
from jax.sharding import PartitionSpec as P

MICRO = 8
SHARD = ("shard_0", "shard_1")


def scatter_axes(value, axes, dim):
    for axis in axes:
        value = lax.psum_scatter(value, axis, scatter_dimension=dim, tiled=True)
    return value


def laid_out(pieces, dim):
    dims = list(pieces.shape[1:])
    dims[dim] *= pieces.shape[0]
    return jnp.moveaxis(pieces, 0, dim).reshape(dims)


def copy_for_each(value, axis):
    size = lax.axis_size(axis)
    return lax.all_to_all(
        jnp.broadcast_to(value[None], (size, *value.shape)), axis, 0, 0, tiled=True
    )


def gather_directly(value, axis, dim):
    return laid_out(copy_for_each(value, axis), dim)


def passed_along(block, axis, distance):
    devices = range(lax.axis_size(axis))
    route = [(i - distance, i) for i in devices if i - distance in devices]
    return lax.ppermute(block, axis, route)


def per_device(activations, top_grad, projection, basis_out, basis_in):
    section_idx = lax.axis_index("section")
    last_section = lax.axis_size("section") - 1
    at_top = section_idx == last_section
    weight_cols = projection[0]
    out_cols = basis_out[0]
    seq_len = top_grad.shape[1]
    feat_loc = top_grad.shape[2]
    eig_rows = out_cols.shape[1]
    scale = 1.0 / jnp.sqrt(jnp.float32(seq_len))
    partial_rot = jnp.einsum(
        "msd,de->mse", activations[0], basis_in[0], preferred_element_type=jnp.float32
    )
    share = scatter_axes(partial_rot, SHARD, 2).astype(jnp.bfloat16)
    rot_in = lax.all_gather(share, SHARD, axis=2, tiled=True)

    def absorb(piece):
        through = jnp.dot(piece, weight_cols, preferred_element_type=jnp.float32)
        rotated = jnp.dot(piece, out_cols, preferred_element_type=jnp.float32)
        return (through, rotated)

    def chain_step(step_index, current):
        micro_idx = step_index - (last_section - section_idx)
        active = jnp.logical_and(micro_idx >= 0, micro_idx < MICRO)
        micro_safe = jnp.clip(micro_idx, 0, MICRO - 1)
        through, rotated = absorb(gather_directly(current, SHARD, 1))
        lower = (current.astype(jnp.float32) + through).astype(jnp.bfloat16)
        received = passed_along(lower, "section", -1)
        next_index = jnp.minimum(step_index + 1, MICRO - 1).astype(jnp.int32)
        next_top = lax.dynamic_index_in_dim(top_grad, next_index, 0, keepdims=False)
        following = jnp.where(at_top, next_top, received)
        return (following, rotated.astype(jnp.bfloat16), active, micro_safe)

    start_grad = jnp.where(at_top, top_grad[0], jnp.zeros((seq_len, feat_loc), jnp.bfloat16))
    total_steps = MICRO + lax.axis_size("section") - 1

    def store_loop(step_index, carry):
        current, stored = carry
        following, rot_out, active, micro_safe = chain_step(step_index, current)
        updated = lax.dynamic_update_index_in_dim(stored, rot_out, micro_safe, 0)
        stored = jnp.where(active, updated, stored)
        return (following, stored)

    start_store = jnp.zeros((MICRO, seq_len, eig_rows), jnp.bfloat16)
    final_grad, stored = lax.fori_loop(0, total_steps, store_loop, (start_grad, start_store))
    product = jnp.einsum("msg,mse->mge", stored, rot_in, preferred_element_type=jnp.float32) * scale
    summed = jnp.sum(product * product, axis=0)
    return (summed / MICRO)[None]


def solution(mesh):
    finer = Mesh(
        mesh.devices.reshape(mesh.shape["section"], 8, 4), ("section", "shard_0", "shard_1")
    )
    in_specs = (
        P("section", None, None, SHARD),
        P(None, None, SHARD),
        P("section", None, SHARD),
        P("section", None, SHARD),
        P("section", SHARD, None),
    )
    out_specs = P("section", SHARD, None)
    return jax.shard_map(
        per_device, mesh=finer, in_specs=in_specs, out_specs=out_specs, check_vma=False
    )
```

profile of v0, /device:TPU:2, one launch (start us, length us, event | category | flops | bytes accessed | tf_op | source)
XLA Modules:
  0.0 578.1 jit_solution(9449147970943247805)
XLA Ops:
  8.1 3.6 fusion.4
  11.8 58.4 %reduce-scatter.3.cloned.1.call-done = f32[8,32,512]{2,1,0:T(8,128)} async-done(((f32[8,32,4096]{2,1,0:T(8,128)}), f32[8,32,512]{2,1,0:T(8,128)}) %reduce-scatter.3.cloned.1.call-update) | async-done | bytes 524304 | tf_op jit(solution)/shard_map/reduce_scatter | solution.py:13
  70.9 22.5 %reduce-scatter.5.cloned.1.call-done = f32[8,32,128]{2,1,0:T(8,128)} async-done(((f32[8,32,512]{2,1,0:T(8,128)}), f32[8,32,128]{2,1,0:T(8,128)}) %reduce-scatter.5.cloned.1.call-update) | async-done | bytes 131088 | tf_op jit(solution)/shard_map/reduce_scatter | solution.py:13
  95.0 470.8 %while.17 = (s32[]{:T(128)}, bf16[32,256]{1,0:T(8,128)(2,1)S(1)}, bf16[8,32,128]{2,1,0:T(8,128)(2,1)S(1)}, pred[]{:T(512)}, bf16[8,32,256]{2,1,0:T(8,128)(2,1)},...) while((s32[]{:T(128)}, bf16[32,256]{1,0:T(8,128)(2,1)S(1)}, ...), condition=%wide.region_1.0_spmd, body=%wide.region_0.0_spmd.sunk | while | flops 201367552 | bytes 19054928 | solution.py:84
  95.9 10.7 %all-to-all-start = ((bf16[32,32,256]{2,1,0:T(8,128)(2,1)}), bf16[32,32,256]{2,1,0:T(8,128)(2,1)S(1)}, u32[]{:S(2)}, u32[]{:S(2)}) async-start(bf16[32,32,256]{2,1,0:T(8,128)(2,1)} %broadcast_in_dim.39), calls=%async_computation | async-start | bytes 1048576 | tf_op jit(solution)/shard_map/while/body/eval_jaxpr/all_to_all | solution.py:25
  106.6 15.2 %all-to-all-done = bf16[32,32,256]{2,1,0:T(8,128)(2,1)S(1)} async-done(((bf16[32,32,256]{2,1,0:T(8,128)(2,1)}), bf16[32,32,256]{2,1,0:T(8,128)(2,1)S(1)}, u32[]{:S(2)}, u32[]{:S(2)}) %all-to-all-start) | async-done | bytes 524320 | tf_op jit(solution)/shard_map/while/body/eval_jaxpr/all_to_all | solution.py:25
  121.8 3.2 fusion.23
  129.6 5.6 all-to-all-start
  135.2 17.5 %all-to-all-done = bf16[32,32,256]{2,1,0:T(8,128)(2,1)S(1)} async-done(((bf16[32,32,256]{2,1,0:T(8,128)(2,1)}), bf16[32,32,256]{2,1,0:T(8,128)(2,1)S(1)}, u32[]{:S(2)}, u32[]{:S(2)}) %all-to-all-start) | async-done | bytes 524320 | tf_op jit(solution)/shard_map/while/body/eval_jaxpr/all_to_all | solution.py:25
  152.8 3.2 fusion.23
  161.8 5.6 all-to-all-start
  167.4 17.9 %all-to-all-done = bf16[32,32,256]{2,1,0:T(8,128)(2,1)S(1)} async-done(((bf16[32,32,256]{2,1,0:T(8,128)(2,1)}), bf16[32,32,256]{2,1,0:T(8,128)(2,1)S(1)}, u32[]{:S(2)}, u32[]{:S(2)}) %all-to-all-start) | async-done | bytes 524320 | tf_op jit(solution)/shard_map/while/body/eval_jaxpr/all_to_all | solution.py:25
  185.4 3.2 fusion.23
  193.6 6.4 %all-to-all-start = ((bf16[32,32,256]{2,1,0:T(8,128)(2,1)}), bf16[32,32,256]{2,1,0:T(8,128)(2,1)S(1)}, u32[]{:S(2)}, u32[]{:S(2)}) async-start(bf16[32,32,256]{2,1,0:T(8,128)(2,1)} %broadcast_in_dim.39), calls=%async_computation | async-start | bytes 1048576 | tf_op jit(solution)/shard_map/while/body/eval_jaxpr/all_to_all | solution.py:25
  200.0 16.8 %all-to-all-done = bf16[32,32,256]{2,1,0:T(8,128)(2,1)S(1)} async-done(((bf16[32,32,256]{2,1,0:T(8,128)(2,1)}), bf16[32,32,256]{2,1,0:T(8,128)(2,1)S(1)}, u32[]{:S(2)}, u32[]{:S(2)}) %all-to-all-start) | async-done | bytes 524320 | tf_op jit(solution)/shard_map/while/body/eval_jaxpr/all_to_all | solution.py:25
  216.9 3.2 fusion.23
  225.4 5.6 all-to-all-start
  231.0 16.3 %all-to-all-done = bf16[32,32,256]{2,1,0:T(8,128)(2,1)S(1)} async-done(((bf16[32,32,256]{2,1,0:T(8,128)(2,1)}), bf16[32,32,256]{2,1,0:T(8,128)(2,1)S(1)}, u32[]{:S(2)}, u32[]{:S(2)}) %all-to-all-start) | async-done | bytes 524320 | tf_op jit(solution)/shard_map/while/body/eval_jaxpr/all_to_all | solution.py:25
  256.5 5.6 all-to-all-start
  262.1 16.1 %all-to-all-done = bf16[32,32,256]{2,1,0:T(8,128)(2,1)S(1)} async-done(((bf16[32,32,256]{2,1,0:T(8,128)(2,1)}), bf16[32,32,256]{2,1,0:T(8,128)(2,1)S(1)}, u32[]{:S(2)}, u32[]{:S(2)}) %all-to-all-start) | async-done | bytes 524320 | tf_op jit(solution)/shard_map/while/body/eval_jaxpr/all_to_all | solution.py:25
  278.2 3.2 fusion.23
  287.5 5.6 all-to-all-start
  293.1 16.1 %all-to-all-done = bf16[32,32,256]{2,1,0:T(8,128)(2,1)S(1)} async-done(((bf16[32,32,256]{2,1,0:T(8,128)(2,1)}), bf16[32,32,256]{2,1,0:T(8,128)(2,1)S(1)}, u32[]{:S(2)}, u32[]{:S(2)}) %all-to-all-start) | async-done | bytes 524320 | tf_op jit(solution)/shard_map/while/body/eval_jaxpr/all_to_all | solution.py:25
  309.2 3.2 fusion.23
  318.5 5.6 all-to-all-start
  324.1 16.1 %all-to-all-done = bf16[32,32,256]{2,1,0:T(8,128)(2,1)S(1)} async-done(((bf16[32,32,256]{2,1,0:T(8,128)(2,1)}), bf16[32,32,256]{2,1,0:T(8,128)(2,1)S(1)}, u32[]{:S(2)}, u32[]{:S(2)}) %all-to-all-start) | async-done | bytes 524320 | tf_op jit(solution)/shard_map/while/body/eval_jaxpr/all_to_all | solution.py:25
  340.2 3.2 fusion.23
  349.5 5.6 all-to-all-start
  355.1 16.1 %all-to-all-done = bf16[32,32,256]{2,1,0:T(8,128)(2,1)S(1)} async-done(((bf16[32,32,256]{2,1,0:T(8,128)(2,1)}), bf16[32,32,256]{2,1,0:T(8,128)(2,1)S(1)}, u32[]{:S(2)}, u32[]{:S(2)}) %all-to-all-start) | async-done | bytes 524320 | tf_op jit(solution)/shard_map/while/body/eval_jaxpr/all_to_all | solution.py:25
  371.2 3.2 fusion.23
  380.5 5.6 all-to-all-start
  386.1 16.1 %all-to-all-done = bf16[32,32,256]{2,1,0:T(8,128)(2,1)S(1)} async-done(((bf16[32,32,256]{2,1,0:T(8,128)(2,1)}), bf16[32,32,256]{2,1,0:T(8,128)(2,1)S(1)}, u32[]{:S(2)}, u32[]{:S(2)}) %all-to-all-start) | async-done | bytes 524320 | tf_op jit(solution)/shard_map/while/body/eval_jaxpr/all_to_all | solution.py:25
  402.3 3.2 fusion.23
  411.5 5.6 all-to-all-start
  417.1 16.1 %all-to-all-done = bf16[32,32,256]{2,1,0:T(8,128)(2,1)S(1)} async-done(((bf16[32,32,256]{2,1,0:T(8,128)(2,1)}), bf16[32,32,256]{2,1,0:T(8,128)(2,1)S(1)}, u32[]{:S(2)}, u32[]{:S(2)}) %all-to-all-start) | async-done | bytes 524320 | tf_op jit(solution)/shard_map/while/body/eval_jaxpr/all_to_all | solution.py:25
  433.3 3.2 fusion.23
  442.6 5.6 all-to-all-start
  448.2 16.1 %all-to-all-done = bf16[32,32,256]{2,1,0:T(8,128)(2,1)S(1)} async-done(((bf16[32,32,256]{2,1,0:T(8,128)(2,1)}), bf16[32,32,256]{2,1,0:T(8,128)(2,1)S(1)}, u32[]{:S(2)}, u32[]{:S(2)}) %all-to-all-start) | async-done | bytes 524320 | tf_op jit(solution)/shard_map/while/body/eval_jaxpr/all_to_all | solution.py:25
  464.3 3.2 fusion.23
  473.6 5.6 all-to-all-start
  479.2 16.1 %all-to-all-done = bf16[32,32,256]{2,1,0:T(8,128)(2,1)S(1)} async-done(((bf16[32,32,256]{2,1,0:T(8,128)(2,1)}), bf16[32,32,256]{2,1,0:T(8,128)(2,1)S(1)}, u32[]{:S(2)}, u32[]{:S(2)}) %all-to-all-start) | async-done | bytes 524320 | tf_op jit(solution)/shard_map/while/body/eval_jaxpr/all_to_all | solution.py:25
  495.3 3.2 fusion.23
  504.6 5.6 all-to-all-start
  510.2 16.1 %all-to-all-done = bf16[32,32,256]{2,1,0:T(8,128)(2,1)S(1)} async-done(((bf16[32,32,256]{2,1,0:T(8,128)(2,1)}), bf16[32,32,256]{2,1,0:T(8,128)(2,1)S(1)}, u32[]{:S(2)}, u32[]{:S(2)}) %all-to-all-start) | async-done | bytes 524320 | tf_op jit(solution)/shard_map/while/body/eval_jaxpr/all_to_all | solution.py:25
  526.3 3.2 fusion.23
  535.6 5.6 all-to-all-start
  541.2 16.1 %all-to-all-done = bf16[32,32,256]{2,1,0:T(8,128)(2,1)S(1)} async-done(((bf16[32,32,256]{2,1,0:T(8,128)(2,1)}), bf16[32,32,256]{2,1,0:T(8,128)(2,1)S(1)}, u32[]{:S(2)}, u32[]{:S(2)}) %all-to-all-start) | async-done | bytes 524320 | tf_op jit(solution)/shard_map/while/body/eval_jaxpr/all_to_all | solution.py:25
  565.8 4.3 multiply_reduce_fusion
  (135 shorter events, 100.0 us)
Async XLA Ops:
  6.5 63.6 %reduce-scatter.3.cloned.1.call-start = ((), (), s32[]{:S(2)}) async-start(), calls=%async_computation.3 | async-start | bytes 4718592 | tf_op jit(solution)/shard_map/reduce_scatter | solution.py:13
  11.7 81.7 %reduce-scatter.5.cloned.1.call-start = ((), (), s32[]{:S(2)}) async-start(), calls=%async_computation.4 | async-start | bytes 655360 | tf_op jit(solution)/shard_map/reduce_scatter | solution.py:13
  70.2 495.6 %all-gather.2.cloned.1.call-start = ((), (), s32[]{:S(2)}) async-start(), calls=%async_computation.5 | async-start | bytes 2162688 | tf_op jit(solution)/shard_map/all_gather | solution.py:54
  95.9 25.9 %all-to-all-start = ((bf16[32,32,256]{2,1,0:T(8,128)(2,1)}), bf16[32,32,256]{2,1,0:T(8,128)(2,1)S(1)}, u32[]{:S(2)}, u32[]{:S(2)}) async-start(bf16[32,32,256]{2,1,0:T(8,128)(2,1)} %broadcast_in_dim.39), calls=%async_computation | async-start | bytes 1048576 | tf_op jit(solution)/shard_map/while/body/eval_jaxpr/all_to_all | solution.py:25
  121.8 4.5 copy-start.1
  125.0 3.1 collective-permute-start
  129.6 23.1 %all-to-all-start = ((bf16[32,32,256]{2,1,0:T(8,128)(2,1)}), bf16[32,32,256]{2,1,0:T(8,128)(2,1)S(1)}, u32[]{:S(2)}, u32[]{:S(2)}) async-start(bf16[32,32,256]{2,1,0:T(8,128)(2,1)} %broadcast_in_dim.39), calls=%async_computation | async-start | bytes 1048576 | tf_op jit(solution)/shard_map/while/body/eval_jaxpr/all_to_all | solution.py:25
  152.8 4.5 copy-start.1
  156.0 4.2 collective-permute-start
  161.8 23.5 %all-to-all-start = ((bf16[32,32,256]{2,1,0:T(8,128)(2,1)}), bf16[32,32,256]{2,1,0:T(8,128)(2,1)S(1)}, u32[]{:S(2)}, u32[]{:S(2)}) async-start(bf16[32,32,256]{2,1,0:T(8,128)(2,1)} %broadcast_in_dim.39), calls=%async_computation | async-start | bytes 1048576 | tf_op jit(solution)/shard_map/while/body/eval_jaxpr/all_to_all | solution.py:25
  185.3 4.5 copy-start.1
  188.5 3.5 collective-permute-start
  193.6 23.2 %all-to-all-start = ((bf16[32,32,256]{2,1,0:T(8,128)(2,1)}), bf16[32,32,256]{2,1,0:T(8,128)(2,1)S(1)}, u32[]{:S(2)}, u32[]{:S(2)}) async-start(bf16[32,32,256]{2,1,0:T(8,128)(2,1)} %broadcast_in_dim.39), calls=%async_computation | async-start | bytes 1048576 | tf_op jit(solution)/shard_map/while/body/eval_jaxpr/all_to_all | solution.py:25
  216.8 4.5 copy-start.1
  220.0 3.8 collective-permute-start
  225.4 21.9 %all-to-all-start = ((bf16[32,32,256]{2,1,0:T(8,128)(2,1)}), bf16[32,32,256]{2,1,0:T(8,128)(2,1)S(1)}, u32[]{:S(2)}, u32[]{:S(2)}) async-start(bf16[32,32,256]{2,1,0:T(8,128)(2,1)} %broadcast_in_dim.39), calls=%async_computation | async-start | bytes 1048576 | tf_op jit(solution)/shard_map/while/body/eval_jaxpr/all_to_all | solution.py:25
  247.4 4.5 copy-start.1
  250.6 4.3 collective-permute-start
  256.5 21.6 %all-to-all-start = ((bf16[32,32,256]{2,1,0:T(8,128)(2,1)}), bf16[32,32,256]{2,1,0:T(8,128)(2,1)S(1)}, u32[]{:S(2)}, u32[]{:S(2)}) async-start(bf16[32,32,256]{2,1,0:T(8,128)(2,1)} %broadcast_in_dim.39), calls=%async_computation | async-start | bytes 1048576 | tf_op jit(solution)/shard_map/while/body/eval_jaxpr/all_to_all | solution.py:25
  278.1 4.5 copy-start.1
  281.3 4.6 collective-permute-start
  287.5 21.7 %all-to-all-start = ((bf16[32,32,256]{2,1,0:T(8,128)(2,1)}), bf16[32,32,256]{2,1,0:T(8,128)(2,1)S(1)}, u32[]{:S(2)}, u32[]{:S(2)}) async-start(bf16[32,32,256]{2,1,0:T(8,128)(2,1)} %broadcast_in_dim.39), calls=%async_computation | async-start | bytes 1048576 | tf_op jit(solution)/shard_map/while/body/eval_jaxpr/all_to_all | solution.py:25
  309.2 4.5 copy-start.1
  312.4 4.6 collective-permute-start
  318.5 21.7 %all-to-all-start = ((bf16[32,32,256]{2,1,0:T(8,128)(2,1)}), bf16[32,32,256]{2,1,0:T(8,128)(2,1)S(1)}, u32[]{:S(2)}, u32[]{:S(2)}) async-start(bf16[32,32,256]{2,1,0:T(8,128)(2,1)} %broadcast_in_dim.39), calls=%async_computation | async-start | bytes 1048576 | tf_op jit(solution)/shard_map/while/body/eval_jaxpr/all_to_all | solution.py:25
  340.2 4.5 copy-start.1
  343.4 4.5 collective-permute-start
  349.5 21.7 %all-to-all-start = ((bf16[32,32,256]{2,1,0:T(8,128)(2,1)}), bf16[32,32,256]{2,1,0:T(8,128)(2,1)S(1)}, u32[]{:S(2)}, u32[]{:S(2)}) async-start(bf16[32,32,256]{2,1,0:T(8,128)(2,1)} %broadcast_in_dim.39), calls=%async_computation | async-start | bytes 1048576 | tf_op jit(solution)/shard_map/while/body/eval_jaxpr/all_to_all | solution.py:25
  371.2 4.5 copy-start.1
  374.4 4.5 collective-permute-start
  380.5 21.7 %all-to-all-start = ((bf16[32,32,256]{2,1,0:T(8,128)(2,1)}), bf16[32,32,256]{2,1,0:T(8,128)(2,1)S(1)}, u32[]{:S(2)}, u32[]{:S(2)}) async-start(bf16[32,32,256]{2,1,0:T(8,128)(2,1)} %broadcast_in_dim.39), calls=%async_computation | async-start | bytes 1048576 | tf_op jit(solution)/shard_map/while/body/eval_jaxpr/all_to_all | solution.py:25
  402.2 4.5 copy-start.1
  405.4 4.5 collective-permute-start
  411.5 21.7 %all-to-all-start = ((bf16[32,32,256]{2,1,0:T(8,128)(2,1)}), bf16[32,32,256]{2,1,0:T(8,128)(2,1)S(1)}, u32[]{:S(2)}, u32[]{:S(2)}) async-start(bf16[32,32,256]{2,1,0:T(8,128)(2,1)} %broadcast_in_dim.39), calls=%async_computation | async-start | bytes 1048576 | tf_op jit(solution)/shard_map/while/body/eval_jaxpr/all_to_all | solution.py:25
  433.3 4.5 copy-start.1
  436.4 4.5 collective-permute-start
  442.6 21.7 %all-to-all-start = ((bf16[32,32,256]{2,1,0:T(8,128)(2,1)}), bf16[32,32,256]{2,1,0:T(8,128)(2,1)S(1)}, u32[]{:S(2)}, u32[]{:S(2)}) async-start(bf16[32,32,256]{2,1,0:T(8,128)(2,1)} %broadcast_in_dim.39), calls=%async_computation | async-start | bytes 1048576 | tf_op jit(solution)/shard_map/while/body/eval_jaxpr/all_to_all | solution.py:25
  464.3 4.5 copy-start.1
  467.5 4.5 collective-permute-start
  473.6 21.7 %all-to-all-start = ((bf16[32,32,256]{2,1,0:T(8,128)(2,1)}), bf16[32,32,256]{2,1,0:T(8,128)(2,1)S(1)}, u32[]{:S(2)}, u32[]{:S(2)}) async-start(bf16[32,32,256]{2,1,0:T(8,128)(2,1)} %broadcast_in_dim.39), calls=%async_computation | async-start | bytes 1048576 | tf_op jit(solution)/shard_map/while/body/eval_jaxpr/all_to_all | solution.py:25
  495.3 4.5 copy-start.1
  498.5 4.5 collective-permute-start
  504.6 21.7 %all-to-all-start = ((bf16[32,32,256]{2,1,0:T(8,128)(2,1)}), bf16[32,32,256]{2,1,0:T(8,128)(2,1)S(1)}, u32[]{:S(2)}, u32[]{:S(2)}) async-start(bf16[32,32,256]{2,1,0:T(8,128)(2,1)} %broadcast_in_dim.39), calls=%async_computation | async-start | bytes 1048576 | tf_op jit(solution)/shard_map/while/body/eval_jaxpr/all_to_all | solution.py:25
  526.3 4.5 copy-start.1
  529.5 4.5 collective-permute-start
  535.6 21.7 %all-to-all-start = ((bf16[32,32,256]{2,1,0:T(8,128)(2,1)}), bf16[32,32,256]{2,1,0:T(8,128)(2,1)S(1)}, u32[]{:S(2)}, u32[]{:S(2)}) async-start(bf16[32,32,256]{2,1,0:T(8,128)(2,1)} %broadcast_in_dim.39), calls=%async_computation | async-start | bytes 1048576 | tf_op jit(solution)/shard_map/while/body/eval_jaxpr/all_to_all | solution.py:25
  557.3 4.5 copy-start.1
  560.5 4.5 collective-permute-start
  (1 other events, 1.6 us)
Sparse Core Ops, SparseCore 0:
  11.8 58.2 reduce-scatter.2
  72.7 20.7 reduce-scatter.4
  95.9 85.5 all-gather.1
where the time goes:
time: 588 us; the launch traced here: 578 us
  waiting for transfers between devices  363 us (62%)
  starting transfers between devices  109 us (19%)
  matrix products  62.1 us (11%)
  local copies, waits for them, and re-layouts  15 us (3%)
  other arithmetic  14.6 us (2%)
  between operations  13.1 us (2%)
    all_to_all x15, waiting for transfers between devices, copy_for_each(): lax.all_to_all(jnp.broadcast_to(value[None], (size, *value.shape)), axis,...  244 us
    all_to_all x15, starting transfers between devices, copy_for_each(): lax.all_to_all(jnp.broadcast_to(value[None], (size, *value.shape)), axis,...  89.5 us
    reduce_scatter x2, waiting for transfers between devices, scatter_axes(): value = lax.psum_scatter(value, axis, scatter_dimension=dim, tiled=True)  80.9 us
    dot_general x15, matrix products, absorb(): through = jnp.dot(piece, weight_cols, preferred_element_type=jnp.float32)  47.5 us
    ppermute x15, waiting for transfers between devices, passed_along(): return lax.ppermute(block, axis, route)  37.8 us
    ppermute x15, starting transfers between devices, passed_along(): return lax.ppermute(block, axis, route)  19.4 us
    broadcast_in_dim x15, local copies, waits for them, and re-layouts, copy_for_each(): jnp.broadcast_to(value[None], (size, *value.shape))  12.8 us
  transfers between devices with their start and end apart: 33, of which 32 were waited for; matrix products, arithmetic and copies ran while one was open for 14% of the time, Pallas kernels for 0%

commit v1 on v0

v1 whole, which is shorter than its diff:
```python
import functools

import jax
import jax.numpy as jnp
from jax import lax
from jax.experimental import pallas as pl
from jax.experimental.pallas import tpu as pltpu
from jax.sharding import Mesh
from jax.sharding import PartitionSpec as P

MESH = pl.DeviceIdType.MESH
SHARD = ("shard_0", "shard_1")
GROUPS = 8


def ring_order(size):
    near = [d for i in range(1, (size + 1) // 2) for d in (i, -i)]
    return [0] + near + ([size // 2] if size % 2 == 0 else [])


def chain_kernel(sections, nz, nx, groups, top, weight, basis, rot, gath, low, acc, accb,
                 z_recv, p_recv, m_recv, f_recv, t_send, z_send, x_send):
    k = lax.axis_index("section")
    z = lax.axis_index("shard_0")
    x = lax.axis_index("shard_1")
    offsets = ring_order(nz)
    width = weight.shape[1]
    right, left = lax.rem(x + 1, nx), lax.rem(x + nx - 1, nx)
    across = lax.rem(x + 2, nx)
    first = k == sections - 1
    inner = k < sections - 1
    passes = k > 0

    def at_z(offset):
        return lax.rem(z + offset + nz, nz)

    def copy(src, dst, send, recv, device):
        return pltpu.make_async_remote_copy(
            src_ref=src, dst_ref=dst, send_sem=send, recv_sem=recv,
            device_id=device, device_id_type=MESH,
        )

    barrier = pltpu.get_barrier_semaphore()

    def greet(device):
        pl.semaphore_signal(barrier, inc=1, device_id=device, device_id_type=MESH)

    greet((k, z, right))
    greet((k, z, left))

    @pl.when(passes)
    def _():
        for offset in offsets:
            greet((k - 1, at_z(offset), x))

    @pl.when(inner)
    def _():
        for offset in offsets:
            greet((k + 1, at_z(offset), x))

    @pl.when(first)
    def _():
        for offset in offsets[1:]:
            greet((k, at_z(offset), x))

    count = 2 + nz * passes.astype(jnp.int32) + nz * inner.astype(jnp.int32)
    pl.semaphore_wait(barrier, count + (nz - 1) * first.astype(jnp.int32))

    @pl.when(first)
    def _():
        def launch(g, carry):
            for i in reversed(range(1, nz)):
                copy(top.at[g], gath.at[g, x, z], t_send.at[g], z_recv.at[g, i],
                     (k, at_z(-offsets[i]), x)).start()
            gath[g, x, z] = top[g]
            return carry
        lax.fori_loop(0, groups, launch, 0)

    def multiply(g, column, table):
        total = None
        for zz in range(nz):
            start = pl.multiple_of((zz * nx + column) * width, width)
            part = jnp.dot(gath[g, column, zz], table[pl.ds(start, width), :],
                           preferred_element_type=jnp.float32)
            total = part if total is None else total + part
        return total

    def group_step(g, carry):
        for i, offset in enumerate(offsets):
            zz = at_z(offset)
            arrival = copy(low.at[g], gath.at[g, x, zz], z_send.at[g], z_recv.at[g, i], (k, z, x))
            if i == 0:
                pl.when(inner)(lambda: arrival.wait_recv())
            else:
                arrival.wait_recv()
            chunk = gath.at[g, x, zz]
            copy(chunk, chunk, x_send.at[g], p_recv.at[g, i], (k, z, right)).start()
            copy(chunk, chunk, x_send.at[g], m_recv.at[g, i], (k, z, left)).start()

        @pl.when(passes)
        def _():
            acc[...] = multiply(g, x, weight)

        for i, offset in enumerate(offsets):
            zz = at_z(offset)
            from_left, from_right = gath.at[g, left, zz], gath.at[g, right, zz]
            copy(from_left, from_left, x_send.at[g], p_recv.at[g, i], (k, z, right)).wait_recv()
            if i % 2 == 0:
                copy(from_left, from_left, x_send.at[g], f_recv.at[g], (k, z, right)).start()
            copy(from_right, from_right, x_send.at[g], m_recv.at[g, i], (k, z, left)).wait_recv()
            if i % 2 == 1:
                copy(from_right, from_right, x_send.at[g], f_recv.at[g], (k, z, left)).start()

        @pl.when(passes)
        def _():
            acc[...] += multiply(g, left, weight) + multiply(g, right, weight)

        far = gath.at[g, across]
        copy(far, far, x_send.at[g], f_recv.at[g], (k, z, right)).wait_recv()

        @pl.when(passes)
        def _():
            through = acc[...] + multiply(g, across, weight)
            low[g] = (gath[g, x, z].astype(jnp.float32) + through).astype(low.dtype)
            for i in reversed(range(nz)):
                copy(low.at[g], gath.at[g, x, z], z_send.at[g], z_recv.at[g, i],
                     (k - 1, at_z(-offsets[i]), x)).start()

        accb[...] = multiply(g, 0, basis) + multiply(g, 1, basis)
        rot[g] = (accb[...] + multiply(g, 2, basis) + multiply(g, 3, basis)).astype(rot.dtype)
        return carry

    lax.fori_loop(0, groups, group_step, 0)

    def drain(g, carry):
        sent = gath.at[g, pl.ds(0, nx - 1)]
        copy(sent, sent, x_send.at[g], f_recv.at[g], (k, z, right)).wait_send()

        @pl.when(passes)
        def _():
            column = gath.at[g, 0]
            copy(column, column, z_send.at[g], f_recv.at[g], (k, z, right)).wait_send()

        @pl.when(first)
        def _():
            column = gath.at[g, 0, pl.ds(0, nz - 1)]
            copy(column, column, t_send.at[g], f_recv.at[g], (k, z, right)).wait_send()
        return carry

    lax.fori_loop(0, groups, drain, 0)


def run_chain(sections, nz, nx, top, weight, basis):
    micro, seq, feat = top.shape
    groups = GROUPS
    rows = micro * seq // groups
    eig = basis.shape[1]
    dma = pltpu.SemaphoreType.DMA
    out = pl.pallas_call(
        functools.partial(chain_kernel, sections, nz, nx, groups),
        out_shape=jax.ShapeDtypeStruct((groups, rows, eig), jnp.bfloat16),
        in_specs=[pl.BlockSpec(memory_space=pltpu.VMEM)] * 3,
        out_specs=pl.BlockSpec(memory_space=pltpu.VMEM),
        scratch_shapes=[
            pltpu.VMEM((groups, nx, nz, rows, feat), jnp.bfloat16),
            pltpu.VMEM((groups, rows, feat), jnp.bfloat16),
            pltpu.VMEM((rows, feat), jnp.float32),
            pltpu.VMEM((rows, eig), jnp.float32),
            dma((groups, nz)), dma((groups, nz)), dma((groups, nz)), dma((groups,)),
            dma((groups,)), dma((groups,)), dma((groups,)),
        ],
        compiler_params=pltpu.CompilerParams(
            collective_id=0, has_side_effects=True, vmem_limit_bytes=40 << 20
        ),
        name="chain",
    )(top.reshape(groups, rows, feat), weight, basis)
    return out.reshape(micro, seq, eig)


def scatter_axes(value, axes, dim):
    for axis in axes:
        value = lax.psum_scatter(value, axis, scatter_dimension=dim, tiled=True)
    return value


def per_device(sections, nz, nx, activations, top_grad, projection, basis_out, basis_in):
    micro, seq_len = top_grad.shape[:2]
    scale = 1.0 / jnp.sqrt(jnp.float32(seq_len))
    partial_rot = jnp.einsum(
        "msd,de->mse", activations[0], basis_in[0], preferred_element_type=jnp.float32
    )
    share = scatter_axes(partial_rot, SHARD, 2).astype(jnp.bfloat16)
    rot_in = lax.all_gather(share, SHARD, axis=2, tiled=True)
    stored = run_chain(sections, nz, nx, top_grad, projection[0], basis_out[0])
    product = jnp.einsum("msg,mse->mge", stored, rot_in, preferred_element_type=jnp.float32) * scale
    summed = jnp.sum(product * product, axis=0)
    return (summed / micro)[None]


def solution(mesh):
    sections = mesh.shape["section"]
    nx = 4
    nz = mesh.shape["shard"] // nx
    finer = Mesh(mesh.devices.reshape(sections, nz, nx), ("section", "shard_0", "shard_1"))
    in_specs = (
        P("section", None, None, SHARD),
        P(None, None, SHARD),
        P("section", None, SHARD),
        P("section", None, SHARD),
        P("section", SHARD, None),
    )
    out_specs = P("section", SHARD, None)
    return jax.shard_map(
        functools.partial(per_device, sections, nz, nx), mesh=finer, in_specs=in_specs,
        out_specs=out_specs, check_vma=False,
    )
```

time: 588 us -> 283 us (0.48); the launches traced: 578 us -> 283 us
  waiting for transfers between devices: 363 us -> 81.7 us
  Pallas kernels: 0 us -> 171 us
  starting transfers between devices: 109 us -> 0.08 us
  matrix products: 62.1 us -> 7.86 us
  other arithmetic: 14.6 us -> 3.04 us
  local copies, waits for them, and re-layouts: 15 us -> 5.37 us
    all_to_all x15 -> x0, waiting for transfers between devices: 244 us -> none  [copy_for_each(): lax.all_to_all(jnp.broadcast_to(value[None], (size, *value.shape)), axis,...]
    pallas_call x0 -> x1, Pallas kernels: none -> 171 us  [run_chain(): pl.pallas_call(functools.partial(chain_kernel, sections, nz, nx, groups),...]
    all_to_all x15 -> x0, starting transfers between devices: 89.5 us -> none  [copy_for_each(): lax.all_to_all(jnp.broadcast_to(value[None], (size, *value.shape)), axis,...]
    dot_general x30 -> x0, matrix products: 54.2 us -> none  [the longest x15 47.5 us: absorb(): through = jnp.dot(piece, weight_cols, preferred_element_type=jnp.float32)]
    ppermute x15 -> x0, waiting for transfers between devices: 37.8 us -> none  [passed_along(): return lax.ppermute(block, axis, route)]
    ppermute x15 -> x0, starting transfers between devices: 19.4 us -> none  [passed_along(): return lax.ppermute(block, axis, route)]
    broadcast_in_dim x16 -> x0, local copies, waits for them, and re-layouts: 12.8 us -> none  [the longest x15 12.8 us: copy_for_each(): jnp.broadcast_to(value[None], (size, *value.shape))]
    select_n x16 -> x0, other arithmetic: 11.6 us -> none  [the longest x15 10.8 us: chain_step(): following = jnp.where(at_top, next_top, received)]
  transfers between devices with their start and end apart: 33 -> 3, of which waited for: 32 -> 2; matrix products, arithmetic and copies ran while one was open for 14% -> 0% of each run, Pallas kernels for 0% -> 61%
where the time goes in v1:
time: 283 us
  Pallas kernels  171 us (60%)
  waiting for transfers between devices  81.7 us (29%)
  between operations  13.1 us (5%)
  matrix products  7.86 us (3%)
  local copies, waits for them, and re-layouts  5.37 us (2%)
  other arithmetic  3.04 us (1%)
    pallas_call x1, Pallas kernels, run_chain(): pl.pallas_call(functools.partial(chain_kernel, sections, nz, nx, groups),...  171 us
    reduce_scatter x2, waiting for transfers between devices, scatter_axes(): value = lax.psum_scatter(value, axis, scatter_dimension=dim, tiled=True)  81.6 us
  transfers between devices with their start and end apart: 3, of which 2 were waited for; matrix products, arithmetic and copies ran while one was open for 0% of the time, Pallas kernels for 61%

profile of v1, /device:TPU:2, one launch (start us, length us, event | category | flops | bytes accessed | tf_op | source)
XLA Modules:
  0.0 282.5 jit_solution(11744034895454311503)
XLA Ops:
  6.5 0.0 copy-start
  6.5 0.0 reduce-scatter.3.cloned.1.call-start
  6.5 1.6 copy-done
  8.1 3.6 %fusion = f32[8,32,4096]{2,1,0:T(8,128)} fusion(bf16[1,256,4096]{2,1,0:T(8,128)(2,1)S(1)} %copy-done, bf16[1,8,32,256]{3,2,1,0:T(8,128)(2,1)} %param.5), kind=kOutput, calls=%fused_computation.1 | convolution fusion | flops 536870912 | bytes 6422528 | tf_op jit(solution)/shard_map/msd,de->mse/dot_general | solution.py:189
  11.7 0.0 copy-start.3
  11.7 0.0 reduce-scatter.3.cloned.1.call-update
  11.7 0.0 reduce-scatter.5.cloned.1.call-start
  11.8 58.4 %reduce-scatter.3.cloned.1.call-done = f32[8,32,512]{2,1,0:T(8,128)} async-done(((f32[8,32,4096]{2,1,0:T(8,128)}), f32[8,32,512]{2,1,0:T(8,128)}) %reduce-scatter.3.cloned.1.call-update) | async-done | bytes 524304 | tf_op jit(solution)/shard_map/reduce_scatter | solution.py:182
  70.1 0.0 reduce-scatter.5.cloned.1.call-update
  70.2 0.0 all-gather.2.cloned.1.call-start
  70.2 23.2 %reduce-scatter.5.cloned.1.call-done = f32[8,32,128]{2,1,0:T(8,128)} async-done(((f32[8,32,512]{2,1,0:T(8,128)}), f32[8,32,128]{2,1,0:T(8,128)}) %reduce-scatter.5.cloned.1.call-update) | async-done | bytes 131088 | tf_op jit(solution)/shard_map/reduce_scatter | solution.py:182
  93.4 1.5 convert_element_type.3
  95.0 0.0 all-gather.2.cloned.1.call-update
  95.0 0.0 copy-done.3
  95.0 0.0 copy-start.1
  95.0 2.2 copy-done.1
  97.2 0.0 copy-start.2
  97.2 1.6 copy-done.2
  98.8 171.3 %chain.1 = bf16[8,32,128]{2,1,0:T(8,128)(2,1)S(1)} custom-call(bf16[8,32,256]{2,1,0:T(8,128)(2,1)S(1)} %copy-done.3, bf16[8192,256]{1,0:T(8,128)(2,1)S(1)} %bitcast.13, bf16[8192,128]{1,0:T(8,128)(2,1)S(1)} %bitcast.14), custom_call_target="tpu_custom_call" | custom-call | tf_op jit(solution)/shard_map/chain/pallas_call | solution.py:159
  270.1 0.0 all-gather.2.cloned.1.call-done
  270.2 4.3 %multiply_reduce_fusion = f32[128,4096]{1,0:T(8,128)S(1)} fusion(bf16[8,32,128]{2,1,0:T(8,128)(2,1)S(1)} %chain.1, bf16[8,32,4096]{2,1,0:T(8,128)(2,1)} %all-gather.2.cloned.1.call-done), kind=kOutput, calls=%fused_computation | convolution fusion | flops 280494080 | bytes 4259840 | tf_op jit(solution)/shard_map/msg,mse->mge/dot_general | solution.py:195
  274.5 1.5 multiply_bitcast_fusion
Async XLA Ops:
  6.5 1.6 copy-start
  6.5 63.6 %reduce-scatter.3.cloned.1.call-start = ((), (), s32[]{:S(2)}) async-start(), calls=%async_computation.2 | async-start | bytes 4718592 | tf_op jit(solution)/shard_map/reduce_scatter | solution.py:182
  11.7 83.3 %copy-start.3 = (bf16[8,32,256]{2,1,0:T(8,128)(2,1)S(1)}, bf16[8,32,256]{2,1,0:T(8,128)(2,1)}, u32[]{:S(2)}) copy-start(bf16[8,32,256]{2,1,0:T(8,128)(2,1)} %top.1) | copy-start | bytes 393220
  11.7 81.7 %reduce-scatter.5.cloned.1.call-start = ((), (), s32[]{:S(2)}) async-start(), calls=%async_computation.3 | async-start | bytes 655360 | tf_op jit(solution)/shard_map/reduce_scatter | solution.py:182
  70.2 200.0 %all-gather.2.cloned.1.call-start = ((), (), s32[]{:S(2)}) async-start(), calls=%async_computation.4 | async-start | bytes 2162688 | tf_op jit(solution)/shard_map/all_gather | solution.py:193
  95.0 2.2 copy-start.1
  97.2 1.6 copy-start.2
Sparse Core Ops, SparseCore 0:
  11.8 58.2 reduce-scatter.2
  72.7 20.7 reduce-scatter.4
  95.9 78.6 all-gather.1

commit v2 on v1

v2 whole, which is shorter than its diff:
```python
import functools

import jax
import jax.numpy as jnp
from jax import lax
from jax.experimental import pallas as pl
from jax.experimental.pallas import tpu as pltpu
from jax.sharding import Mesh
from jax.sharding import PartitionSpec as P

MESH = pl.DeviceIdType.MESH
SHARD = ("shard_0", "shard_1")
GROUPS = 16
PAIR = 2
EARLY_SCATTER = 4
EARLY_GATHER = 4
VMEM_LIMIT = 56 << 20


def ring_order(size):
    near = [d for i in range(1, (size + 1) // 2) for d in (i, -i)]
    return [0] + near + ([size // 2] if size % 2 == 0 else [])


def fused_kernel(sections, nz, nx, groups, micro, act_hbm, top_hbm, weight_hbm, basis_hbm, in_hbm, out,
                 act, top, weight, basis, basis_in, gath, low, acc, rot, rot_t,
                 part, far_in, near_in, z_in, rot_in, load,
                 z_recv, p_recv, m_recv, f_recv, t_send, z_send, x_send,
                 rf_recv, rn_recv, rz_recv, rf_send, rn_send, rz_send,
                 az_recv, ap_recv, am_recv, af_recv, az_send, ax_send):
    k = lax.axis_index("section")
    z = lax.axis_index("shard_0")
    x = lax.axis_index("shard_1")
    loads = [
        pltpu.make_async_copy(src, dst, load.at[i])
        for i, (src, dst) in enumerate(
            ((top_hbm, top), (act_hbm, act), (in_hbm, basis_in), (weight_hbm, weight), (basis_hbm, basis))
        )
    ]
    for copy_in in loads:
        copy_in.start()
    offsets = ring_order(nz)
    spread = offsets[::-1]
    eig = basis.shape[1]
    width = weight.shape[1]
    right, left = lax.rem(x + 1, nx), lax.rem(x + nx - 1, nx)
    across = lax.rem(x + 2, nx)
    first = k == sections - 1
    inner = k < sections - 1
    passes = k > 0

    def at_z(offset):
        return lax.rem(z + offset + nz, nz)

    def copy(src, dst, send, recv, device):
        return pltpu.make_async_remote_copy(
            src_ref=src, dst_ref=dst, send_sem=send, recv_sem=recv,
            device_id=device, device_id_type=MESH,
        )

    barrier = pltpu.get_barrier_semaphore()

    def greet(device):
        pl.semaphore_signal(barrier, inc=1, device_id=device, device_id_type=MESH)

    for column in (right, left, across):
        greet((k, z, column))
    for offset in offsets[1:]:
        greet((k, at_z(offset), x))

    @pl.when(passes)
    def _():
        for offset in offsets:
            greet((k - 1, at_z(offset), x))

    @pl.when(inner)
    def _():
        for offset in offsets:
            greet((k + 1, at_z(offset), x))

    count = nx + nz - 2 + nz * passes.astype(jnp.int32) + nz * inner.astype(jnp.int32)
    pl.semaphore_wait(barrier, count)
    loads[0].wait()

    @pl.when(first)
    def _():
        def launch(g, carry):
            for i in reversed(range(1, nz)):
                copy(top.at[g], gath.at[g, x, z], t_send.at[g], z_recv.at[g, i],
                     (k, at_z(-offsets[i]), x)).start()
            gath[g, x, z] = top[g]
            return carry
        lax.fori_loop(0, groups, launch, 0)

    def multiply(g, column, table):
        total = None
        for zz in range(nz):
            start = pl.multiple_of((zz * nx + column) * width, width)
            part = jnp.dot(gath[g, column, zz], table[pl.ds(start, width), :],
                           preferred_element_type=jnp.float32)
            total = part if total is None else total + part
        return total

    def relay(g):
        for i, offset in enumerate(offsets):
            zz = at_z(offset)
            arrival = copy(low.at[g], gath.at[g, x, zz], z_send.at[g], z_recv.at[g, i], (k, z, x))
            if i == 0:
                pl.when(inner)(lambda: arrival.wait_recv())
            else:
                arrival.wait_recv()
            chunk = gath.at[g, x, zz]
            copy(chunk, chunk, x_send.at[g], f_recv.at[g], (k, z, across)).start()
            copy(chunk, chunk, x_send.at[g], p_recv.at[g], (k, z, right)).start()
            copy(chunk, chunk, x_send.at[g], m_recv.at[g], (k, z, left)).start()

    def finish(g):
        @pl.when(passes)
        def _():
            acc[...] = multiply(g, x, weight)

        for column, arrived in ((left, p_recv), (right, m_recv)):
            whole = gath.at[g, column]
            copy(whole, whole, x_send.at[g], arrived.at[g], (k, z, right)).wait_recv()

        @pl.when(passes)
        def _():
            acc[...] += multiply(g, left, weight) + multiply(g, right, weight)

        far = gath.at[g, across]
        copy(far, far, x_send.at[g], f_recv.at[g], (k, z, right)).wait_recv()

        @pl.when(passes)
        def _():
            through = acc[...] + multiply(g, across, weight)
            low[g] = (gath[g, x, z].astype(jnp.float32) + through).astype(low.dtype)
            for i in reversed(range(nz)):
                copy(low.at[g], gath.at[g, x, z], z_send.at[g], z_recv.at[g, i],
                     (k - 1, at_z(-offsets[i]), x)).start()

    def rotate(g, size):
        total = None
        for column in range(nx):
            for zz in range(nz):
                lhs = gath[pl.ds(g, size), column, zz]
                lhs = lhs.reshape(lhs.shape[0] * lhs.shape[1], width)
                part = jnp.dot(lhs, basis[(zz * nx + column) * width : (zz * nx + column + 1) * width, :],
                               preferred_element_type=jnp.float32)
                total = part if total is None else total + part
        rot[pl.ds(g, size)] = total.astype(rot.dtype).reshape(size, rot.shape[1], rot.shape[2])

    def group_step(g, carry):
        pl.when(g + 1 < groups)(lambda: relay(g + 1))
        finish(g)
        pl.when(lax.rem(g, PAIR) == PAIR - 1)(lambda: rotate(g - (PAIR - 1), PAIR))
        return carry

    def chain():
        relay(0)
        loads[3].wait()
        loads[4].wait()
        lax.fori_loop(0, groups, group_step, 0)

    def product(owner, zz):
        start = pl.multiple_of((owner * nz + zz) * eig, eig)
        piece = jnp.dot(act[...], basis_in[:, pl.ds(start, eig)], preferred_element_type=jnp.float32)
        part[owner, zz] = piece.astype(part.dtype)

    def reduce_scatter():
        loads[1].wait()
        loads[2].wait()
        for i, offset in enumerate(spread):
            zz = at_z(offset)
            product(across, zz)
            copy(part.at[across, zz], far_in.at[i], rf_send, rf_recv.at[i],
                 (k, z, left if i % 2 == 0 else right)).start()
        for i, offset in enumerate(spread):
            zz = at_z(offset)
            product(left, zz)
            product(right, zz)
            if i % 2 == 0:
                copy(part.at[right, zz], near_in.at[0, i], rn_send, rn_recv.at[0, i], (k, z, right)).start()
            else:
                copy(part.at[left, zz], near_in.at[1, i], rn_send, rn_recv.at[1, i], (k, z, left)).start()
        for i, offset in enumerate(spread):
            zz = at_z(offset)
            product(x, zz)
            copy(far_in.at[i], far_in.at[i], rf_send, rf_recv.at[i], (k, z, left)).wait_recv()
            if i % 2 == 0:
                part[left, zz] = add(part[left, zz], far_in[i])
                copy(part.at[left, zz], near_in.at[1, i], rn_send, rn_recv.at[1, i], (k, z, left)).start()
            else:
                part[right, zz] = add(part[right, zz], far_in[i])
                copy(part.at[right, zz], near_in.at[0, i], rn_send, rn_recv.at[0, i], (k, z, right)).start()
        for i, offset in enumerate(spread):
            zz = at_z(offset)
            for side in range(2):
                arrived = near_in.at[side, i]
                copy(arrived, arrived, rn_send, rn_recv.at[side, i], (k, z, left)).wait_recv()
            part[x, zz] = add(part[x, zz], near_in[0, i], near_in[1, i])
            if offset != 0:
                copy(part.at[x, zz], z_in.at[i], rz_send, rz_recv.at[i], (k, zz, x)).start()
        total = part[x, z].astype(jnp.float32)
        for i, offset in enumerate(spread):
            if offset != 0:
                copy(z_in.at[i], z_in.at[i], rz_send, rz_recv.at[i], (k, z, left)).wait_recv()
                total = total + z_in[i].astype(jnp.float32)
        rot_in[x, z] = total.astype(rot_in.dtype)

    def add(*terms):
        total = terms[0].astype(jnp.float32)
        for term in terms[1:]:
            total = total + term.astype(jnp.float32)
        return total.astype(part.dtype)

    def all_gather():
        mine = rot_in.at[x, z]
        for i in reversed(range(1, nz)):
            copy(mine, mine, az_send, az_recv.at[i], (k, at_z(-offsets[i]), x)).start()
        for i, offset in enumerate(offsets):
            piece = rot_in.at[x, at_z(offset)]
            if i > 0:
                copy(piece, piece, az_send, az_recv.at[i], (k, z, right)).wait_recv()
            copy(piece, piece, ax_send, ap_recv.at[i], (k, z, right)).start()
            copy(piece, piece, ax_send, am_recv.at[i], (k, z, left)).start()
        for i, offset in enumerate(offsets):
            zz = at_z(offset)
            from_left, from_right = rot_in.at[left, zz], rot_in.at[right, zz]
            copy(from_left, from_left, ax_send, ap_recv.at[i], (k, z, right)).wait_recv()
            if i % 2 == 0:
                copy(from_left, from_left, ax_send, af_recv, (k, z, right)).start()
            copy(from_right, from_right, ax_send, am_recv.at[i], (k, z, left)).wait_recv()
            if i % 2 == 1:
                copy(from_right, from_right, ax_send, af_recv, (k, z, left)).start()
        whole = rot_in.at[across]
        copy(whole, whole, ax_send, af_recv, (k, z, left)).wait_recv()

    scatter_stage = jnp.where(k < EARLY_SCATTER, 0, 2)
    gather_stage = jnp.where(k < EARLY_GATHER, 0, 2)

    def stage(index, carry):
        pl.when(index == scatter_stage)(reduce_scatter)
        pl.when(index == gather_stage)(all_gather)
        pl.when(index == 1)(chain)
        return carry

    lax.fori_loop(0, 3, stage, 0)

    seq = groups * low.shape[1] // micro
    per = groups // micro
    for m in range(micro):
        tokens = rot[m * per : (m + 1) * per].reshape(seq, eig)
        rot_t[m] = (tokens.astype(jnp.float32) * (1.0 / 16.0)).T.astype(rot_t.dtype)

    def square(step, carry):
        column, half = step // (nz // 2), lax.rem(step, nz // 2)
        total = None
        for m in range(micro):
            rows = pl.ds(m * seq, seq)
            rhs = jnp.concatenate(
                [rot_in[column, 2 * half, rows], rot_in[column, 2 * half + 1, rows]], axis=1
            )
            value = jnp.dot(rot_t[m], rhs, preferred_element_type=jnp.float32)
            total = value * value if total is None else total + value * value
        out[:, pl.ds(pl.multiple_of(step * 2 * eig, 2 * eig), 2 * eig)] = total
        return carry

    lax.fori_loop(0, nx * nz // 2, square, 0)

    for pieces, sem in (
        (part.at[0], rf_send), (part.at[pl.ds(0, 2)], rn_send), (part.at[0, pl.ds(0, nz - 1)], rz_send),
        (part.at[0, pl.ds(0, nz - 1)], az_send), (part.at[pl.ds(0, 3)], ax_send),
    ):
        copy(pieces, pieces, sem, af_recv, (k, z, right)).wait_send()

    def drain(g, carry):
        sent = gath.at[g, pl.ds(0, nx - 1)]
        copy(sent, sent, x_send.at[g], f_recv.at[g], (k, z, right)).wait_send()

        @pl.when(passes)
        def _():
            column = gath.at[g, 0]
            copy(column, column, z_send.at[g], f_recv.at[g], (k, z, right)).wait_send()

        @pl.when(first)
        def _():
            column = gath.at[g, 0, pl.ds(0, nz - 1)]
            copy(column, column, t_send.at[g], f_recv.at[g], (k, z, right)).wait_send()
        return carry

    lax.fori_loop(0, groups, drain, 0)


def run_fused(sections, nz, nx, act, top, weight, basis, basis_in):
    micro, seq, feat = top.shape
    groups = GROUPS
    tokens = micro * seq
    rows = tokens // groups
    eig = basis.shape[1]
    half = jnp.bfloat16
    dma = pltpu.SemaphoreType.DMA
    return pl.pallas_call(
        functools.partial(fused_kernel, sections, nz, nx, groups, micro),
        out_shape=jax.ShapeDtypeStruct((eig, nx * nz * eig), jnp.float32),
        in_specs=[pl.BlockSpec(memory_space=pl.ANY)] * 5,
        out_specs=pl.BlockSpec(memory_space=pltpu.VMEM),
        scratch_shapes=[
            pltpu.VMEM((tokens, feat), half),
            pltpu.VMEM((groups, rows, feat), half),
            pltpu.VMEM(weight.shape, half),
            pltpu.VMEM(basis.shape, half),
            pltpu.VMEM(basis_in.shape, half),
            pltpu.VMEM((groups, nx, nz, rows, feat), half),
            pltpu.VMEM((groups, rows, feat), half),
            pltpu.VMEM((rows, feat), jnp.float32),
            pltpu.VMEM((groups, rows, eig), half),
            pltpu.VMEM((micro, eig, seq), half),
            pltpu.VMEM((nx, nz, tokens, eig), half),
            pltpu.VMEM((nz, tokens, eig), half),
            pltpu.VMEM((2, nz, tokens, eig), half),
            pltpu.VMEM((nz, tokens, eig), half),
            pltpu.VMEM((nx, nz, tokens, eig), half),
            dma((5,)),
            dma((groups, nz)), dma((groups,)), dma((groups,)), dma((groups,)),
            dma((groups,)), dma((groups,)), dma((groups,)),
            dma((nz,)), dma((2, nz)), dma((nz,)), dma, dma, dma,
            dma((nz,)), dma((nz,)), dma((nz,)), dma, dma, dma,
        ],
        compiler_params=pltpu.CompilerParams(
            collective_id=0, has_side_effects=True, vmem_limit_bytes=VMEM_LIMIT
        ),
        name="fused",
    )(act.reshape(tokens, feat), top.reshape(groups, rows, feat), weight, basis, basis_in)


def per_device(sections, nz, nx, activations, top_grad, projection, basis_out, basis_in):
    return run_fused(
        sections, nz, nx, activations[0], top_grad, projection[0], basis_out[0], basis_in[0]
    )[None]


def solution(mesh):
    sections = mesh.shape["section"]
    nx = 4
    nz = mesh.shape["shard"] // nx
    finer = Mesh(mesh.devices.reshape(sections, nz, nx), ("section", "shard_0", "shard_1"))
    in_specs = (
        P("section", None, None, SHARD),
        P(None, None, SHARD),
        P("section", None, SHARD),
        P("section", None, SHARD),
        P("section", SHARD, None),
    )
    out_specs = P("section", SHARD, None)
    return jax.shard_map(
        functools.partial(per_device, sections, nz, nx), mesh=finer, in_specs=in_specs,
        out_specs=out_specs, check_vma=False,
    )
```

time: 283 us -> 157 us (0.55)
  waiting for transfers between devices: 81.7 us -> 0 us
  Pallas kernels: 171 us -> 154 us
  between operations: 13.1 us -> 0.01 us
  matrix products: 7.86 us -> 0 us
  other arithmetic: 3.04 us -> 0 us
    reduce_scatter x2 -> x0, waiting for transfers between devices: 81.6 us -> none  [scatter_axes(): value = lax.psum_scatter(value, axis, scatter_dimension=dim, tiled=True)]
    pallas_call x1, Pallas kernels: 171 us -> 154 us  [run_fused(): pl.pallas_call(functools.partial(fused_kernel, sections, nz, nx, groups,...]
    dot_general x2 -> x0, matrix products: 7.86 us -> none  [the longest x1 4.3 us: per_device(): jnp.einsum('msg,mse->mge', stored, rot_in, preferred_element_type=jnp.flo...]
  transfers between devices with their start and end apart: 3 -> 0, of which waited for: 2 -> 0; matrix products, arithmetic and copies ran while one was open for 0% -> 0% of each run, Pallas kernels for 61% -> 0%
where the time goes in v2:
time: 157 us
  Pallas kernels  154 us (98%)
  local copies, waits for them, and re-layouts  3.11 us (2%)
    pallas_call x1, Pallas kernels, run_fused(): pl.pallas_call(functools.partial(fused_kernel, sections, nz, nx, groups,...  154 us

profile of v2, /device:TPU:2, one launch (start us, length us, event | category | flops | bytes accessed | tf_op | source)
XLA Modules:
  0.0 156.9 jit_solution(949135572689176624)
XLA Ops:
  0.0 153.7 %fused.1 = f32[128,4096]{1,0:T(8,128)} custom-call(bf16[256,256]{1,0:T(8,128)(2,1)} %bitcast.10, bf16[16,16,256]{2,1,0:T(8,128)(2,1)} %bitcast.11, bf16[8192,256]{1,0:T(8,128)(2,1)} %bitcast.7, bf16[8192,128]{1,0:T(8,128)(2,1)} %bitcast.8, bf16[256,4096]{1,0:T(8,128)(2,1)} %bitcast.9), custom_call_target="tpu_custom_call" | custom-call | tf_op jit(solution)/shard_map/fused/pallas_call | solution.py:302
  153.8 3.1 %copy.7 = f32[1,128,4096]{2,1,0:T(8,128)} copy(f32[1,128,4096]{2,1,0:T(8,128)} %bitcast.6) | data formatting | bytes 4194304

commit v3 on v2

--- a/solution.py
+++ b/solution.py
@@ -11,10 +11,10 @@
 MESH = pl.DeviceIdType.MESH
 SHARD = ("shard_0", "shard_1")
 GROUPS = 16
-PAIR = 2
-EARLY_SCATTER = 4
-EARLY_GATHER = 4
-VMEM_LIMIT = 56 << 20
+EARLY_SCATTER = 6
+EARLY_GATHER = 2
+AHEAD = 2
+VMEM_LIMIT = 26 << 20
 
 
 def ring_order(size):
@@ -43,6 +43,10 @@
     spread = offsets[::-1]
     eig = basis.shape[1]
     width = weight.shape[1]
+    per = groups // micro
+    seq = per * low.shape[1]
+    scatter_stage = jnp.where(k < EARLY_SCATTER, 0, 2)
+    gather_stage = jnp.where(k < EARLY_GATHER, 0, 2)
     right, left = lax.rem(x + 1, nx), lax.rem(x + nx - 1, nx)
     across = lax.rem(x + 2, nx)
     first = k == sections - 1
@@ -149,14 +153,36 @@
                 total = part if total is None else total + part
         rot[pl.ds(g, size)] = total.astype(rot.dtype).reshape(size, rot.shape[1], rot.shape[2])
 
+    def rotated(m, column, half):
+        rows = pl.ds(pl.multiple_of(m * seq, seq), seq)
+        rhs = jnp.concatenate(
+            [rot_in[column, 2 * half, rows], rot_in[column, 2 * half + 1, rows]], axis=1
+        )
+        return jnp.dot(rot_t[m], rhs, preferred_element_type=jnp.float32)
+
+    def square_one(m):
+        for step in range(nx * nz // 2):
+            value = rotated(m, step // (nz // 2), step % (nz // 2))
+            columns = slice(step * 2 * eig, (step + 1) * 2 * eig)
+            before = jnp.where(m > 0, out[:, columns], 0.0)
+            out[:, columns] = before + value * value
+
     def group_step(g, carry):
-        pl.when(g + 1 < groups)(lambda: relay(g + 1))
+        pl.when(g + AHEAD < groups)(lambda: relay(g + AHEAD))
         finish(g)
-        pl.when(lax.rem(g, PAIR) == PAIR - 1)(lambda: rotate(g - (PAIR - 1), PAIR))
+
+        @pl.when(lax.rem(g, per) == per - 1)
+        def _():
+            m = g // per
+            rotate(m * per, per)
+            tokens = rot[pl.ds(m * per, per)].reshape(seq, eig)
+            rot_t[m] = (tokens.astype(jnp.float32) * (1.0 / 16.0)).T.astype(rot_t.dtype)
+            pl.when(gather_stage == 0)(lambda: square_one(m))
         return carry
 
     def chain():
-        relay(0)
+        for early in range(AHEAD):
+            relay(early)
         loads[3].wait()
         loads[4].wait()
         lax.fori_loop(0, groups, group_step, 0)
@@ -235,9 +261,6 @@
         whole = rot_in.at[across]
         copy(whole, whole, ax_send, af_recv, (k, z, left)).wait_recv()
 
-    scatter_stage = jnp.where(k < EARLY_SCATTER, 0, 2)
-    gather_stage = jnp.where(k < EARLY_GATHER, 0, 2)
-
     def stage(index, carry):
         pl.when(index == scatter_stage)(reduce_scatter)
         pl.when(index == gather_stage)(all_gather)
@@ -246,26 +269,17 @@
 
     lax.fori_loop(0, 3, stage, 0)
 
-    seq = groups * low.shape[1] // micro
-    per = groups // micro
-    for m in range(micro):
-        tokens = rot[m * per : (m + 1) * per].reshape(seq, eig)
-        rot_t[m] = (tokens.astype(jnp.float32) * (1.0 / 16.0)).T.astype(rot_t.dtype)
-
-    def square(step, carry):
-        column, half = step // (nz // 2), lax.rem(step, nz // 2)
-        total = None
-        for m in range(micro):
-            rows = pl.ds(m * seq, seq)
-            rhs = jnp.concatenate(
-                [rot_in[column, 2 * half, rows], rot_in[column, 2 * half + 1, rows]], axis=1
-            )
-            value = jnp.dot(rot_t[m], rhs, preferred_element_type=jnp.float32)
-            total = value * value if total is None else total + value * value
-        out[:, pl.ds(pl.multiple_of(step * 2 * eig, 2 * eig), 2 * eig)] = total
-        return carry
-
-    lax.fori_loop(0, nx * nz // 2, square, 0)
+    @pl.when(gather_stage > 0)
+    def _():
+        def square(step, carry):
+            total = None
+            for m in range(micro):
+                value = rotated(m, step // (nz // 2), lax.rem(step, nz // 2))
+                total = value * value if total is None else total + value * value
+            out[:, pl.ds(pl.multiple_of(step * 2 * eig, 2 * eig), 2 * eig)] = total
+            return carry
+
+        lax.fori_loop(0, nx * nz // 2, square, 0)
 
     for pieces, sem in (
         (part.at[0], rf_send), (part.at[pl.ds(0, 2)], rn_send), (part.at[0, pl.ds(0, nz - 1)], rz_send),
@@ -302,7 +316,7 @@
     return pl.pallas_call(
         functools.partial(fused_kernel, sections, nz, nx, groups, micro),
         out_shape=jax.ShapeDtypeStruct((eig, nx * nz * eig), jnp.float32),
-        in_specs=[pl.BlockSpec(memory_space=pl.ANY)] * 5,
+        in_specs=[pl.BlockSpec(memory_space=pltpu.HBM)] * 5,
         out_specs=pl.BlockSpec(memory_space=pltpu.VMEM),
         scratch_shapes=[
             pltpu.VMEM((tokens, feat), half),
@@ -330,7 +344,8 @@
             collective_id=0, has_side_effects=True, vmem_limit_bytes=VMEM_LIMIT
         ),
         name="fused",
-    )(act.reshape(tokens, feat), top.reshape(groups, rows, feat), weight, basis, basis_in)
+    )(*(pltpu.with_memory_space_constraint(a, pltpu.HBM) for a in (
+        act.reshape(tokens, feat), top.reshape(groups, rows, feat), weight, basis, basis_in)))
 
 
 def per_device(sections, nz, nx, activations, top_grad, projection, basis_out, basis_in):

time: 157 us -> 142 us (0.904); the launches traced: 157 us -> 139 us
  Pallas kernels: 154 us -> 138 us
  local copies, waits for them, and re-layouts: 3.11 us -> 1.32 us
    pallas_call x1, Pallas kernels: 154 us -> 138 us  [run_fused(): pl.pallas_call(functools.partial(fused_kernel, sections, nz, nx, groups,...]
    unnamed x1, local copies, waits for them, and re-layouts: 3.11 us -> 1.32 us
where the time goes in v3:
time: 142 us; the launch traced here: 139 us
  Pallas kernels  138 us (97%)
    pallas_call x1, Pallas kernels, run_fused(): pl.pallas_call(functools.partial(fused_kernel, sections, nz, nx, groups,...  138 us

profile of v3, /device:TPU:2, one launch (start us, length us, event | category | flops | bytes accessed | tf_op | source)
XLA Modules:
  0.0 138.9 jit_solution(4070708404739908836)
XLA Ops:
  0.0 137.5 %fused.1 = f32[128,4096]{1,0:T(8,128)S(1)} custom-call(bf16[256,256]{1,0:T(8,128)(2,1)} %bitcast.10, bf16[16,16,256]{2,1,0:T(8,128)(2,1)} %bitcast.11, bf16[8192,256]{1,0:T(8,128)(2,1)} %bitcast.7, bf16[8192,128]{1,0:T(8,128)(2,1)} %bitcast.8, bf16[256,4096]{1,0:T(8,128)(2,1)} %bitcast.9), custom_call_target="tpu_custom_call" | custom-call | tf_op jit(solution)/shard_map/fused/pallas_call | solution.py:316
  137.5 1.3 copy.7

commit v4 on v3

--- a/solution.py
+++ b/solution.py
@@ -14,7 +14,9 @@
 EARLY_SCATTER = 6
 EARLY_GATHER = 2
 AHEAD = 2
+LAUNCH = 4
 VMEM_LIMIT = 26 << 20
+PAIRED = {0: 1, 1: 1, 2: -1}
 
 
 def ring_order(size):
@@ -25,7 +27,7 @@
 def fused_kernel(sections, nz, nx, groups, micro, act_hbm, top_hbm, weight_hbm, basis_hbm, in_hbm, out,
                  act, top, weight, basis, basis_in, gath, low, acc, rot, rot_t,
                  part, far_in, near_in, z_in, rot_in, load,
-                 z_recv, p_recv, m_recv, f_recv, t_send, z_send, x_send,
+                 z_recv, b_recv, p_recv, m_recv, f_recv, t_send, z_send, x_send,
                  rf_recv, rn_recv, rz_recv, rf_send, rn_send, rz_send,
                  az_recv, ap_recv, am_recv, af_recv, az_send, ax_send):
     k = lax.axis_index("section")
@@ -67,34 +69,56 @@
     def greet(device):
         pl.semaphore_signal(barrier, inc=1, device_id=device, device_id_type=MESH)
 
+    paired = {i: side for i, side in PAIRED.items() if i < nz}
+    targets = sorted({(-offsets[i] % nz, side) for i, side in paired.items()})
+    sources = sorted({(offsets[i] % nz, -side) for i, side in paired.items()})
+    within = sorted({pair for pair in targets + sources if pair[0] != 0})
+
+    def beside(side):
+        return right if side > 0 else left
+
     for column in (right, left, across):
         greet((k, z, column))
     for offset in offsets[1:]:
         greet((k, at_z(offset), x))
+    for offset, side in within:
+        greet((k, at_z(offset), beside(side)))
 
     @pl.when(passes)
     def _():
         for offset in offsets:
             greet((k - 1, at_z(offset), x))
+        for offset, side in targets:
+            greet((k - 1, at_z(offset), beside(side)))
 
     @pl.when(inner)
     def _():
         for offset in offsets:
             greet((k + 1, at_z(offset), x))
-
-    count = nx + nz - 2 + nz * passes.astype(jnp.int32) + nz * inner.astype(jnp.int32)
+        for offset, side in sources:
+            greet((k + 1, at_z(offset), beside(side)))
+
+    count = nx + nz - 2 + len(within)
+    count = count + (nz + len(targets)) * passes.astype(jnp.int32)
+    count = count + (nz + len(sources)) * inner.astype(jnp.int32)
     pl.semaphore_wait(barrier, count)
     loads[0].wait()
 
-    @pl.when(first)
-    def _():
-        def launch(g, carry):
-            for i in reversed(range(1, nz)):
-                copy(top.at[g], gath.at[g, x, z], t_send.at[g], z_recv.at[g, i],
-                     (k, at_z(-offsets[i]), x)).start()
-            gath[g, x, z] = top[g]
-            return carry
-        lax.fori_loop(0, groups, launch, 0)
+    def push(block, g, sent, section, start):
+        for i in reversed(range(nz)):
+            row = at_z(-offsets[i])
+            if i >= start:
+                copy(block, gath.at[g, x, z], sent, z_recv.at[g, i], (section, row, x)).start()
+            if i in paired:
+                copy(block, gath.at[g, x, z], sent, b_recv.at[g, i],
+                     (section, row, beside(paired[i]))).start()
+
+    def launch(g):
+        push(top.at[g], g, t_send.at[g], k, 1)
+        gath[g, x, z] = top[g]
+
+    for early in range(LAUNCH):
+        pl.when(first)(lambda early=early: launch(early))
 
     def multiply(g, column, table):
         total = None
@@ -114,17 +138,26 @@
             else:
                 arrival.wait_recv()
             chunk = gath.at[g, x, zz]
-            copy(chunk, chunk, x_send.at[g], f_recv.at[g], (k, z, across)).start()
-            copy(chunk, chunk, x_send.at[g], p_recv.at[g], (k, z, right)).start()
-            copy(chunk, chunk, x_send.at[g], m_recv.at[g], (k, z, left)).start()
+            if i not in paired:
+                copy(chunk, chunk, x_send.at[g], f_recv.at[g], (k, z, across)).start()
+            if paired.get(i, -1) < 0:
+                copy(chunk, chunk, x_send.at[g], p_recv.at[g], (k, z, right)).start()
+            if paired.get(i, 1) > 0:
+                copy(chunk, chunk, x_send.at[g], m_recv.at[g], (k, z, left)).start()
+            if i in paired:
+                side = paired[i]
+                near = gath.at[g, beside(-side), zz]
+                copy(near, near, x_send.at[g], b_recv.at[g, i], (k, z, right)).wait_recv()
+                copy(near, near, x_send.at[g], f_recv.at[g], (k, z, beside(side))).start()
 
     def finish(g):
         @pl.when(passes)
         def _():
             acc[...] = multiply(g, x, weight)
 
-        for column, arrived in ((left, p_recv), (right, m_recv)):
-            whole = gath.at[g, column]
+        rights = sum(side > 0 for side in paired.values())
+        for column, arrived, ready in ((left, p_recv, rights), (right, m_recv, len(paired) - rights)):
+            whole = gath.at[g, column, pl.ds(0, nz - ready)]
             copy(whole, whole, x_send.at[g], arrived.at[g], (k, z, right)).wait_recv()
 
         @pl.when(passes)
@@ -138,9 +171,7 @@
         def _():
             through = acc[...] + multiply(g, across, weight)
             low[g] = (gath[g, x, z].astype(jnp.float32) + through).astype(low.dtype)
-            for i in reversed(range(nz)):
-                copy(low.at[g], gath.at[g, x, z], z_send.at[g], z_recv.at[g, i],
-                     (k - 1, at_z(-offsets[i]), x)).start()
+            push(low.at[g], g, z_send.at[g], k - 1, 0)
 
     def rotate(g, size):
         total = None
@@ -169,6 +200,7 @@
 
     def group_step(g, carry):
         pl.when(g + AHEAD < groups)(lambda: relay(g + AHEAD))
+        pl.when(first & (g + LAUNCH < groups))(lambda: launch(g + LAUNCH))
         finish(g)
 
         @pl.when(lax.rem(g, per) == per - 1)
@@ -239,6 +271,21 @@
             total = total + term.astype(jnp.float32)
         return total.astype(part.dtype)
 
+    def run(body):
+        lax.fori_loop(0, nz // 2, body, 0)
+
+    def square_column(column):
+        def square(half, carry):
+            total = None
+            for m in range(micro):
+                value = rotated(m, column, half)
+                total = value * value if total is None else total + value * value
+            start = pl.multiple_of((column * nz + 2 * half) * eig, 2 * eig)
+            out[:, pl.ds(start, 2 * eig)] = total
+            return carry
+
+        pl.when(gather_stage > 0)(lambda: run(square))
+
     def all_gather():
         mine = rot_in.at[x, z]
         for i in reversed(range(1, nz)):
@@ -258,8 +305,11 @@
             copy(from_right, from_right, ax_send, am_recv.at[i], (k, z, left)).wait_recv()
             if i % 2 == 1:
                 copy(from_right, from_right, ax_send, af_recv, (k, z, left)).start()
+        for column in (x, left, right):
+            square_column(column)
         whole = rot_in.at[across]
         copy(whole, whole, ax_send, af_recv, (k, z, left)).wait_recv()
+        square_column(across)
 
     def stage(index, carry):
         pl.when(index == scatter_stage)(reduce_scatter)
@@ -269,18 +319,6 @@
 
     lax.fori_loop(0, 3, stage, 0)
 
-    @pl.when(gather_stage > 0)
-    def _():
-        def square(step, carry):
-            total = None
-            for m in range(micro):
-                value = rotated(m, step // (nz // 2), lax.rem(step, nz // 2))
-                total = value * value if total is None else total + value * value
-            out[:, pl.ds(pl.multiple_of(step * 2 * eig, 2 * eig), 2 * eig)] = total
-            return carry
-
-        lax.fori_loop(0, nx * nz // 2, square, 0)
-
     for pieces, sem in (
         (part.at[0], rf_send), (part.at[pl.ds(0, 2)], rn_send), (part.at[0, pl.ds(0, nz - 1)], rz_send),
         (part.at[0, pl.ds(0, nz - 1)], az_send), (part.at[pl.ds(0, 3)], ax_send),
@@ -288,18 +326,15 @@
         copy(pieces, pieces, sem, af_recv, (k, z, right)).wait_send()
 
     def drain(g, carry):
-        sent = gath.at[g, pl.ds(0, nx - 1)]
-        copy(sent, sent, x_send.at[g], f_recv.at[g], (k, z, right)).wait_send()
-
-        @pl.when(passes)
-        def _():
-            column = gath.at[g, 0]
-            copy(column, column, z_send.at[g], f_recv.at[g], (k, z, right)).wait_send()
-
-        @pl.when(first)
-        def _():
-            column = gath.at[g, 0, pl.ds(0, nz - 1)]
-            copy(column, column, t_send.at[g], f_recv.at[g], (k, z, right)).wait_send()
+        def sent(sem, *sizes):
+            for columns, rows in sizes:
+                if columns and rows:
+                    block = gath.at[g, pl.ds(0, columns), pl.ds(0, rows)]
+                    copy(block, block, sem.at[g], f_recv.at[g], (k, z, right)).wait_send()
+
+        sent(x_send, (3, nz - len(paired)), (2, len(paired)))
+        pl.when(passes)(lambda: sent(z_send, (1, nz), (1, len(paired))))
+        pl.when(first)(lambda: sent(t_send, (1, nz - 1), (1, len(paired))))
         return carry
 
     lax.fori_loop(0, groups, drain, 0)
@@ -335,7 +370,7 @@
             pltpu.VMEM((nz, tokens, eig), half),
             pltpu.VMEM((nx, nz, tokens, eig), half),
             dma((5,)),
-            dma((groups, nz)), dma((groups,)), dma((groups,)), dma((groups,)),
+            dma((groups, nz)), dma((groups, nz)), dma((groups,)), dma((groups,)), dma((groups,)),
             dma((groups,)), dma((groups,)), dma((groups,)),
             dma((nz,)), dma((2, nz)), dma((nz,)), dma, dma, dma,
             dma((nz,)), dma((nz,)), dma((nz,)), dma, dma, dma,

time: 142 us -> 137 us (0.965); the launches traced: 139 us -> 137 us
  Pallas kernels: 138 us -> 136 us
    pallas_call x1, Pallas kernels: 138 us -> 136 us  [run_fused(): pl.pallas_call(functools.partial(fused_kernel, sections, nz, nx, groups,...]
where the time goes in v4:
time: 137 us
  Pallas kernels  136 us (99%)
    pallas_call x1, Pallas kernels, run_fused(): pl.pallas_call(functools.partial(fused_kernel, sections, nz, nx, groups,...  136 us

profile of v4, /device:TPU:2, one launch (start us, length us, event | category | flops | bytes accessed | tf_op | source)
XLA Modules:
  0.0 137.4 jit_solution(17163735620361546189)
XLA Ops:
  0.0 136.1 %fused.1 = f32[128,4096]{1,0:T(8,128)S(1)} custom-call(bf16[256,256]{1,0:T(8,128)(2,1)} %bitcast.10, bf16[16,16,256]{2,1,0:T(8,128)(2,1)} %bitcast.11, bf16[8192,256]{1,0:T(8,128)(2,1)} %bitcast.7, bf16[8192,128]{1,0:T(8,128)(2,1)} %bitcast.8, bf16[256,4096]{1,0:T(8,128)(2,1)} %bitcast.9), custom_call_target="tpu_custom_call" | custom-call | tf_op jit(solution)/shard_map/fused/pallas_call | solution.py:351
  136.1 1.3 copy.7

commit v5 on v4

--- a/solution.py
+++ b/solution.py
@@ -11,7 +11,7 @@
 MESH = pl.DeviceIdType.MESH
 SHARD = ("shard_0", "shard_1")
 GROUPS = 16
-EARLY_SCATTER = 6
+EARLY_SCATTER = 4
 EARLY_GATHER = 2
 AHEAD = 2
 LAUNCH = 4

time: 137 us -> 136 us (level); the launches traced: 137 us -> 134 us
  Pallas kernels: 136 us -> 133 us
    pallas_call x1, Pallas kernels: 136 us -> 133 us  [run_fused(): pl.pallas_call(functools.partial(fused_kernel, sections, nz, nx, groups,...]
where the time goes in v5:
time: 136 us; the launch traced here: 134 us
  Pallas kernels  133 us (98%)
    pallas_call x1, Pallas kernels, run_fused(): pl.pallas_call(functools.partial(fused_kernel, sections, nz, nx, groups,...  133 us

profile of v5, /device:TPU:2, one launch (start us, length us, event | category | flops | bytes accessed | tf_op | source)
XLA Modules:
  0.0 133.9 jit_solution(6671855224611873382)
XLA Ops:
  0.0 132.6 %fused.1 = f32[128,4096]{1,0:T(8,128)S(1)} custom-call(bf16[256,256]{1,0:T(8,128)(2,1)} %bitcast.10, bf16[16,16,256]{2,1,0:T(8,128)(2,1)} %bitcast.11, bf16[8192,256]{1,0:T(8,128)(2,1)} %bitcast.7, bf16[8192,128]{1,0:T(8,128)(2,1)} %bitcast.8, bf16[256,4096]{1,0:T(8,128)(2,1)} %bitcast.9), custom_call_target="tpu_custom_call" | custom-call | tf_op jit(solution)/shard_map/fused/pallas_call | solution.py:351
  132.6 1.3 copy.7
